TPU v7x, 32 devices: a whole 2x2x4 slice. The times are simulated.
32 devices in a mesh: group: 4 (over y, x), dev: 8 (over z, core).
Axes of the slice: x: 2, y: 2, z: 4, core: 2. Of those that a mesh axis runs over, the one named last changes fastest.
Arguments:
- density: float32 [32, 320, 128], P(('group', 'dev')), may hold values from 0.5 to 2
- velocity: float32 [3, 32, 320, 128], P(None, ('group', 'dev')), may hold values from -0.75 to 0.75
- pressure: float32 [32, 320, 128], P(('group', 'dev')), may hold values from 0.5 to 2
- rbf_blocks: bfloat16 [2048, 128, 128], P(('group', 'dev')), may hold values from -0.5 to 0.5
- correlation: int32 [2048, 128], P(('group', 'dev')), may hold values from 0 to 319
- normals: float32 [2048, 3, 128], P(('group', 'dev')), may hold values from -6 to 6
- routes: int32 [2048, 1], P(('group', 'dev')), may hold values from 0 to 31; in each aligned block of 64 rows (0 to 63, 64 to 127, ...) at most 4 rows name the same one
- targets: int32 [2048], P(('group', 'dev')), may hold values from 0 to 31
- stiffness: bfloat16 [1024, 128, 128], P(('group', 'dev')), may hold values from -0.35 to 2.35
- coupling: bfloat16 [1024, 128, 128], P(('group', 'dev')), may hold values from -0.5 to 0.5
- inverse_diag: float32 [1024, 3, 128], P(('group', 'dev')), may hold values from 0.5 to 1.5
- displacement: float32 [1024, 3, 128], P(('group', 'dev')), may hold values from -6 to 6
- diff_res: float32 [8, 1024, 3, 128], P(None, ('group', 'dev')), may hold values from -2 to 2
- diff_disp: float32 [8, 1024, 3, 128], P(None, ('group', 'dev')), may hold values from -2.4 to 2.4
Outputs:
- fluid_next: float32 [5, 32, 320, 128], P(None, ('group', 'dev'))
- disp_next: float32 [1024, 3, 128], P(('group', 'dev'))
- wall_motion: float32 [2048, 3, 128], P(('group', 'dev'))
Inputs may be any that keep to these rules, and one draw needn't show every extreme that they name: `routes`: among the 64 blocks of one device at most 4 name the same owner, and some device names one owner exactly 4 times.
All inputs are finite; a program needn't handle non-finite values.
Results may differ from a plain program's by a relative error of at most 0.0004.
The roundings to bfloat16 on the way count: a program that leaves them out, or rounds other values in their place, can miss the bound.
Values may be sent and summed in bfloat16 or wider, within the bound.
A program may use at most 64 MiB of HBM per device.

v0:
```python
import jax
import jax.numpy as jnp
from jax import lax
from jax.sharding import PartitionSpec as P

ratio_heat = 1.4
step_ratio = 0.03


def extended(value, sides, width):
    for axis, dim in sides:
        peers, length = (lax.axis_size(axis), value.shape[dim])
        up = [(i, (i + 1) % peers) for i in range(peers)]
        down = [(j, i) for i, j in up]
        last = lax.slice_in_dim(value, length - width, length, axis=dim)
        leading = lax.slice_in_dim(value, 0, width, axis=dim)
        before = lax.ppermute(last, axis, up)
        after = lax.ppermute(leading, axis, down)
        value = jnp.concatenate([before, value, after], axis=dim)
    return value


def shifted(block, axis, distance):
    devices = range(lax.axis_size(axis))
    route = [(i - distance, i) for i in devices if i - distance in devices]
    return lax.ppermute(block, axis, route)


def euler_flux(state, normal_axis):
    dens = state[0]
    vel = state[1:4] / dens
    press = (ratio_heat - 1.0) * (state[4] - 0.5 * dens * jnp.sum(vel * vel, axis=0))
    normal_speed = vel[normal_axis]
    rows = [dens * normal_speed]
    for comp in range(3):
        moment = state[1 + comp] * normal_speed
        if comp == normal_axis:
            moment = moment + press
        rows.append(moment)
    rows.append((state[4] + press) * normal_speed)
    wave_speed = jnp.abs(normal_speed) + jnp.sqrt(ratio_heat * press / dens)
    return (jnp.stack(rows, axis=0), wave_speed)


def rusanov(left_state, right_state, normal_axis):
    flux_left, speed_left = euler_flux(left_state, normal_axis)
    flux_right, speed_right = euler_flux(right_state, normal_axis)
    return 0.5 * (flux_left + flux_right) - 0.5 * jnp.maximum(speed_left, speed_right) * (
        right_state - left_state
    )


def conserve(density, velocity, pressure):
    energy = pressure / (ratio_heat - 1.0) + 0.5 * density * jnp.sum(velocity * velocity, axis=0)
    return jnp.concatenate([density[None], density[None] * velocity, energy[None]], axis=0)


def advance(padded, conserved):
    face_x = rusanov(padded[:, :-1], padded[:, 1:], 0)
    divergence = face_x[:, 1:] - face_x[:, :-1]
    face_y = rusanov(conserved, jnp.roll(conserved, -1, axis=2), 1)
    divergence = divergence + face_y - jnp.roll(face_y, 1, axis=2)
    mirror_sign = jnp.array([1.0, 1.0, 1.0, -1.0, 1.0], dtype=conserved.dtype)[:, None, None, None]
    padded_z = jnp.concatenate(
        [conserved[..., :1] * mirror_sign, conserved, conserved[..., -1:]], axis=3
    )
    face_z = rusanov(padded_z[..., :-1], padded_z[..., 1:], 2)
    divergence = divergence + face_z[..., 1:] - face_z[..., :-1]
    return conserved - step_ratio * divergence


def wall_pressure(state):
    bottom = state[..., 0]
    return (ratio_heat - 1.0) * (
        bottom[4] - 0.5 * jnp.sum(bottom[1:4] * bottom[1:4], axis=0) / bottom[0]
    )


def cho_apply(gram, projected):
    factor = jnp.linalg.cholesky(gram)
    middle = lax.linalg.triangular_solve(factor, projected[:, None], left_side=True, lower=True)
    return lax.linalg.triangular_solve(
        factor, middle, left_side=True, lower=True, transpose_a=True
    )[:, 0]


def on_device(
    density,
    velocity,
    pressure,
    rbf_blocks,
    correlation,
    normals,
    routes,
    targets,
    stiffness,
    coupling,
    inverse_diag,
    displacement,
    diff_res,
    diff_disp,
):
    conserved = conserve(density, velocity, pressure)
    padded = extended(conserved, ((("group", "dev"), 1),), 1)
    fluid_next = advance(padded, conserved)
    wall_row = wall_pressure(fluid_next).reshape(-1)
    weighted = (wall_row[correlation][:, None, :] * normals).astype(jnp.bfloat16)
    block_loads = jnp.einsum(
        "bci,bij->bcj", weighted, rbf_blocks, preferred_element_type=jnp.float32
    )
    blocks = block_loads.shape[0]
    width_row = block_loads.shape[1] * block_loads.shape[2]
    peer_count = lax.axis_size(("group", "dev"))
    capacity = max(2, 2 * blocks // peer_count)
    slot_count = peer_count * capacity
    target_dev = routes[:, 0]
    member = (target_dev[:, None] == jnp.arange(peer_count, dtype=jnp.int32)[None, :]).astype(
        jnp.int32
    )
    position = jnp.sum((jnp.cumsum(member, axis=0) - member) * member, axis=1)
    slot_id = target_dev * capacity + position
    send_loads = (
        jnp.zeros((slot_count, width_row), jnp.float32)
        .at[slot_id]
        .set(block_loads.reshape(blocks, width_row))
    )
    send_tag = (
        jnp.full((slot_count,), -1.0, jnp.float32).at[slot_id].set(targets.astype(jnp.float32))
    )
    got_loads, got_tag = (
        lax.all_to_all(
            send_loads.reshape(peer_count, capacity, width_row),
            ("group", "dev"),
            split_axis=0,
            concat_axis=0,
            tiled=True,
        ),
        lax.all_to_all(
            send_tag.reshape(peer_count, capacity),
            ("group", "dev"),
            split_axis=0,
            concat_axis=0,
            tiled=True,
        ),
    )
    got_loads = got_loads.reshape(slot_count, width_row)
    got_tag = got_tag.reshape(slot_count)
    solid_count = displacement.shape[0]
    selector = (got_tag[None, :] == jnp.arange(solid_count, dtype=jnp.float32)[:, None]).astype(
        jnp.float32
    )
    solid_load = jnp.dot(
        selector, got_loads, precision=lax.Precision.HIGHEST, preferred_element_type=jnp.float32
    ).reshape(displacement.shape)
    disp_half = displacement.astype(jnp.bfloat16)
    prior_block = shifted(disp_half[-1:], ("group", "dev"), 1)
    earlier = jnp.concatenate([prior_block, disp_half[:-1]], axis=0)
    solid_res = jnp.einsum("bcj,bij->bci", disp_half, stiffness, preferred_element_type=jnp.float32)
    solid_res = (
        solid_res
        + jnp.einsum("bcj,bij->bci", earlier, coupling, preferred_element_type=jnp.float32)
        - solid_load
    )
    coupling_res = -inverse_diag * solid_res
    projected_local = jnp.einsum(
        "mbcj,bcj->m", diff_res, coupling_res, precision=lax.Precision.HIGHEST
    )
    gram_local = jnp.einsum("mbcj,nbcj->mn", diff_res, diff_res, precision=lax.Precision.HIGHEST)
    gram_matrix, projected = lax.psum((gram_local, projected_local), ("group", "dev"))
    mixing = -cho_apply(gram_matrix, projected)
    disp_next = (
        displacement
        + coupling_res
        + jnp.einsum("mbcj,m->bcj", diff_disp, mixing, precision=lax.Precision.HIGHEST)
    )
    reply_rows = disp_next.astype(jnp.bfloat16).reshape(solid_count, width_row)
    replies = jnp.dot(
        selector.T.astype(jnp.bfloat16), reply_rows, preferred_element_type=jnp.float32
    ).astype(jnp.bfloat16)
    returned = lax.all_to_all(
        replies.reshape(peer_count, capacity, width_row),
        ("group", "dev"),
        split_axis=0,
        concat_axis=0,
        tiled=True,
    )
    picked = returned.reshape(slot_count, width_row)[slot_id].reshape(block_loads.shape)
    wall_motion = jnp.einsum("bij,bcj->bci", rbf_blocks, picked, preferred_element_type=jnp.float32)
    return (fluid_next, disp_next, wall_motion)


def solution(mesh):
    placed = (
        P(("group", "dev"), None, None),
        P(None, ("group", "dev"), None, None),
        P(("group", "dev"), None, None),
        P(("group", "dev"), None, None),
        P(("group", "dev"), None),
        P(("group", "dev"), None, None),
        P(("group", "dev"), None),
        P(("group", "dev")),
        P(("group", "dev"), None, None),
        P(("group", "dev"), None, None),
        P(("group", "dev"), None, None),
        P(("group", "dev"), None, None),
        P(None, ("group", "dev"), None, None),
        P(None, ("group", "dev"), None, None),
    )
    return jax.shard_map(
        on_device,
        mesh=mesh,
        in_specs=placed,
        out_specs=(
            P(None, ("group", "dev"), None, None),
            P(("group", "dev"), None, None),
            P(("group", "dev"), None, None),
        ),
        check_vma=False,
    )
```

profile of v0, /device:TPU:0, one launch (start us, length us, event | category | flops | bytes accessed | tf_op | source)
XLA Modules:
  0.0 170.8 jit_solution(8857625696449889218)
XLA Ops:
  0.7 1.4 multiply_reduce_fusion.5
  2.0 0.7 bitcast_dynamic-update-slice_fusion.1
  2.8 0.7 fusion.55
  3.4 0.7 fusion.54
  4.2 0.9 pad_maximum_fusion.3
  5.1 6.4 %collective-permute-start.1 = (f32[5,1,320,128]{3,2,1,0:T(8,128)}, f32[5,1,320,128]{3,2,1,0:T(8,128)}, u32[]{:S(2)}, u32[]{:S(2)}) collective-permute-start(f32[5,1,320,128]{3,2,1,0:T(8,128)} %pad_maximum_fusion.3), channel_id=1, source_target_pairs={{1,0},{2,1},{3,2},{4,3},{5,4},{6,5},{7,6},{8,7},{9,8},{10,9},{11,1... | collective-permute-start | bytes 2457608 | tf_op jit(solution)/shard_map/ppermute | solution.py:18
  11.9 0.8 scatter_custom_fusion
  12.7 0.7 all_to_all.12
  13.4 5.7 %all-to-all-start = ((f32[32,1,4]{2,1,0:T(1,128)}), f32[32,1,4]{2,1,0:T(1,128)S(1)}, u32[]{:S(2)}, u32[]{:S(2)}) async-start(f32[32,1,4]{2,1,0:T(1,128)} %bitcast.30), calls=%async_computation | async-start | bytes 32768 | tf_op jit(solution)/shard_map/all_to_all | solution.py:138
  19.1 0.7 slice.284
  19.8 1.2 slice.283
  21.1 1.7 fusion.107
  24.4 0.7 fusion.50
  25.2 0.8 copy-done.4
  26.3 0.8 bitcast_dynamic-update-slice_fusion
  27.1 1.4 fusion.6
  28.6 0.6 multiply_subtract_fusion
  29.2 2.4 %collective-permute-done = f32[5,1,320,128]{3,2,1,0:T(8,128)} collective-permute-done((f32[5,1,320,128]{3,2,1,0:T(8,128)}, f32[5,1,320,128]{3,2,1,0:T(8,128)}, u32[]{:S(2)}, u32[]{:S(2)}) %collective-permute-start) | collective-permute-done | bytes 819232 | tf_op jit(solution)/shard_map/ppermute | solution.py:17
  31.6 1.7 %pad_maximum_fusion.1 = (f32[5,2,320,128]{3,2,1,0:T(8,128)S(1)}, f32[5,2,320,128]{3,2,1,0:T(8,128)S(1)}) fusion(f32[5,1,320,128]{3,2,1,0:T(8,128)} %collective-permute-done.1, f32[1,1,320,128]{3,2,1,0:T(8,128)S(1)} %bitcast.216, f32[3,1,320,128]{3,2,1,0:T(8,128)S(1)} %get-tuple-element.48, f32[1,1,320,128]{3,2,1,0:T(8,128)S(1)} %bitcast.209, ...), kind=kLoop, calls=%fused_computation.12 | loop fusion | flops 2457600 | bytes 5734400 | tf_op jit(solution)/shard_map/concatenate | solution.py:19
  34.6 1.7 %multiply_subtract_fusion.1 = f32[5,2,320,128]{3,2,1,0:T(8,128)S(1)} fusion(f32[5,2,320,128]{3,2,1,0:T(8,128)S(1)} %multiply_dynamic-update-slice_fusion.6, f32[5,2,320,128]{3,2,1,0:T(8,128)S(1)} %multiply_dynamic-update-slice_fusion.4, f32[2,320,128]{2,1,0:T(8,128)S(1)} %get-tuple-element.18, f32[5,1,320,128]{3,2,1,0:T(8,128)} %collective-permute-done.1, ...), kind=kLoop, calls=%fused_computation.16 | loop fusion | flops 4505600 | bytes 7700480 | tf_op jit(solution)/shard_map/sub | solution.py:48
  37.0 0.5 copy-done.2
  37.6 51.2 %gather_fusion = f32[8192]{0:T(1024)S(1)} fusion(f32[320]{0:T(512)S(1)} %subtract_multiply_fusion, s32[8192]{0:T(1024)S(1)} %fusion.78), kind=kCustom, calls=%fused_computation | custom fusion | bytes 98304 | tf_op jit(solution)/shard_map/gather | solution.py:107
  88.9 1.3 fusion.74
  90.2 1.8 %scatter_custom_fusion.1 = f32[128,384]{1,0:T(8,128)} fusion(s32[64]{0:T(128)} %copy-done.14, f32[8,8,3,128]{3,2,1,0:T(4,128)} %bitcast.223, f32[]{:T(128)} %constant.80.clone.1), kind=kCustom, calls=%fused_computation.164 | custom fusion | bytes 328192 | tf_op jit(solution)/shard_map/scatter | solution.py:125
  92.0 1.7 reshape.784
  93.7 3.6 %all-to-all-start.1 = ((f32[32,4,384]{2,1,0:T(4,128)}), f32[32,4,384]{2,1,0:T(4,128)}, u32[]{:S(2)}, u32[]{:S(2)}) async-start(f32[32,4,384]{2,1,0:T(4,128)} %reshape.784), calls=%async_computation.1 | async-start | bytes 393216 | tf_op jit(solution)/shard_map/all_to_all | solution.py:131
  97.2 0.8 copy.93
  98.6 2.7 %collective-permute-start.2 = (bf16[1,3,128]{2,1,0:T(4,128)(2,1)}, bf16[1,3,128]{2,1,0:T(4,128)(2,1)}, u32[]{:S(2)}, u32[]{:S(2)}) collective-permute-start(bf16[1,3,128]{2,1,0:T(4,128)(2,1)} %slice.318), channel_id=1, source_target_pairs={{0,1},{1,2},{2,3},{3,4},{4,5},{5,6},{6,7},{7,8},{8,9},{9,10},{10,1... | collective-permute-start | bytes 2312 | tf_op jit(solution)/shard_map/ppermute | solution.py:26
  101.3 0.6 slice.319
  101.9 1.6 convolution_bitcast_fusion
  103.5 1.3 fusion.108
  105.3 0.6 reduce.20
  106.1 1.0 reshape.785
  107.4 1.9 %fusion.1 = f32[32,3,128]{2,1,0:T(4,128)S(1)} fusion(f32[32,3,128]{2,1,0:T(4,128)} %fusion.108, bf16[32,128,128]{2,1,0:T(8,128)(2,1)} %param.24, f32[32,3,128]{2,0,1:T(8,128)S(1)} %fusion.87, f32[32,3,128]{2,0,1:T(8,128)} %param.25, bf16[31,3,128]{2,1,0:T(4,128)(2,1)} %slice.319, bf16[1,3,128]{2,1,0:T(4,128)(2,1)} %collective-permute-done.2), kind=kOutput, calls=%fused_computation.20 | convolution fusion | flops 3244032 | bytes 1269760 | tf_op jit(solution)/shard_map/bcj,bij->bci/dot_general | solution.py:161
  109.4 1.1 convolution_bitcast_fusion.3
  110.5 40.0 %all-reduce = (f32[8,8]{0,1:T(8,128)S(1)}, f32[8]{0:T(128)S(1)}) all-reduce(f32[8,8]{0,1:T(8,128)S(1)} %copy-done.12, f32[8]{0:T(128)S(1)} %convolution_bitcast_fusion.3), channel_id=1, replica_groups=mesh['group'=4,'dev'=8] {'group','dev'}, use_global_device_ids=true, to_apply=%region_12.13 | all-reduce | flops 72 | bytes 576 | tf_op jit(solution)/shard_map/psum | solution.py:169
  150.6 0.7 cholesky.16
  151.4 0.6 compare_reduce_fusion
  152.0 0.6 fusion.90
  152.7 0.6 custom-call.8
  153.6 0.7 fusion.14
  154.5 0.7 reshape.787
  155.2 5.3 %all-to-all-start.2 = ((bf16[32,4,384]{2,1,0:T(4,128)(2,1)}), bf16[32,4,384]{2,1,0:T(4,128)(2,1)S(1)}, u32[]{:S(2)}, u32[]{:S(2)}) async-start(bf16[32,4,384]{2,1,0:T(4,128)(2,1)} %reshape.787), calls=%async_computation.2 | async-start | bytes 196608 | tf_op jit(solution)/shard_map/all_to_all | solution.py:180
  160.5 0.6 copy.55
  161.1 7.1 %all-to-all-done.2 = bf16[32,4,384]{2,1,0:T(4,128)(2,1)S(1)} async-done(((bf16[32,4,384]{2,1,0:T(4,128)(2,1)}), bf16[32,4,384]{2,1,0:T(4,128)(2,1)S(1)}, u32[]{:S(2)}, u32[]{:S(2)}) %all-to-all-start.2) | async-done | bytes 98336 | tf_op jit(solution)/shard_map/all_to_all | solution.py:180
  168.3 0.7 gather_fusion.1
  169.0 1.2 fusion.109
  170.2 0.7 copy.56
  (98 shorter events, 6.7 us)
Async XLA Ops:
  0.6 88.2 %copy-start = (bf16[64,128,128]{2,1,0:T(8,128)(2,1)S(1)}, bf16[64,128,128]{2,1,0:T(8,128)(2,1)}, u32[]{:S(2)}) copy-start(bf16[64,128,128]{2,1,0:T(8,128)(2,1)} %param.18) | copy-start | bytes 6291460
  0.6 1.4 copy-start.1
  0.7 2.8 %copy-start.9 = (f32[1,320,128]{2,1,0:T(8,128)S(1)}, f32[1,320,128]{2,1,0:T(8,128)}, u32[]{:S(2)}) copy-start(f32[1,320,128]{2,1,0:T(8,128)} %param.17) | copy-start | bytes 491524
  2.0 3.1 %copy-start.3 = (f32[320,128]{1,0:T(8,128)}, f32[320,128]{1,0:T(8,128)S(1)}, u32[]{:S(2)}) copy-start(f32[320,128]{1,0:T(8,128)S(1)} %get-tuple-element.29) | copy-start | bytes 491524
  2.7 8.8 %copy-start.13 = (s32[64,1]{0,1:T(1,128)S(1)}, s32[64,1]{0,1:T(1,128)}, u32[]{:S(2)}) copy-start(s32[64,1]{0,1:T(1,128)} %param.21) | copy-start | bytes 772
  3.4 8.4 %copy-start.17 = (s32[64]{0:T(128)S(1)}, s32[64]{0:T(128)}, u32[]{:S(2)}) copy-start(s32[64]{0:T(128)} %param.22) | copy-start | bytes 772
  4.2 16.9 %copy-start.16 = (f32[5]{0:T(128)S(1)}, f32[5]{0:T(128)}, u32[]{:S(2)}) copy-start(f32[5]{0:T(128)} %constant.91.clone) | copy-start | bytes 64
  5.1 24.1 %collective-permute-start.1 = (f32[5,1,320,128]{3,2,1,0:T(8,128)}, f32[5,1,320,128]{3,2,1,0:T(8,128)}, u32[]{:S(2)}, u32[]{:S(2)}) collective-permute-start(f32[5,1,320,128]{3,2,1,0:T(8,128)} %pad_maximum_fusion.3), channel_id=1, source_target_pairs={{1,0},{2,1},{3,2},{4,3},{5,4},{6,5},{7,6},{8,7},{9,8},{10,9},{11,1... | collective-permute-start | bytes 2457608 | tf_op jit(solution)/shard_map/ppermute | solution.py:18
  11.5 20.1 %collective-permute-start = (f32[5,1,320,128]{3,2,1,0:T(8,128)}, f32[5,1,320,128]{3,2,1,0:T(8,128)}, u32[]{:S(2)}, u32[]{:S(2)}) collective-permute-start(f32[5,1,320,128]{3,2,1,0:T(8,128)} %pad_maximum_fusion.3), channel_id=1, source_target_pairs={{0,1},{1,2},{2,3},{3,4},{4,5},{5,6},{6,7},{7,8},{8,9},{9,10},{10,1... | collective-permute-start | bytes 2457608 | tf_op jit(solution)/shard_map/ppermute | solution.py:17
  11.9 10.9 %copy-start.14 = (s32[64]{0:T(128)}, s32[64]{0:T(128)S(1)}, u32[]{:S(2)}) copy-start(s32[64]{0:T(128)S(1)} %fusion.94) | copy-start | bytes 772
  13.4 80.2 %all-to-all-start = ((f32[32,1,4]{2,1,0:T(1,128)}), f32[32,1,4]{2,1,0:T(1,128)S(1)}, u32[]{:S(2)}, u32[]{:S(2)}) async-start(f32[32,1,4]{2,1,0:T(1,128)} %bitcast.30), calls=%async_computation | async-start | bytes 32768 | tf_op jit(solution)/shard_map/all_to_all | solution.py:138
  25.1 0.9 copy-start.4
  27.1 1.5 copy-start.11
  36.7 0.9 copy-start.2
  37.6 51.2 %copy-start.10 = (f32[64,3,128]{2,0,1:T(8,128)S(1)}, f32[64,3,128]{2,0,1:T(8,128)}, u32[]{:S(2)}) copy-start(f32[64,3,128]{2,0,1:T(8,128)} %param.20) | copy-start | bytes 294916
  88.9 13.1 %copy-start.5 = (f32[8,32,3,128]{3,1,2,0:T(8,128)S(1)}, f32[8,32,3,128]{3,1,2,0:T(8,128)}, u32[]{:S(2)}) copy-start(f32[8,32,3,128]{3,1,2,0:T(8,128)} %param.27) | copy-start | bytes 1179652
  88.9 14.6 %copy-start.6 = (bf16[32,128,128]{2,1,0:T(8,128)(2,1)S(1)}, bf16[32,128,128]{2,1,0:T(8,128)(2,1)}, u32[]{:S(2)}) copy-start(bf16[32,128,128]{2,1,0:T(8,128)(2,1)} %param.23) | copy-start | bytes 3145732
  93.7 12.4 %all-to-all-start.1 = ((f32[32,4,384]{2,1,0:T(4,128)}), f32[32,4,384]{2,1,0:T(4,128)}, u32[]{:S(2)}, u32[]{:S(2)}) async-start(f32[32,4,384]{2,1,0:T(4,128)} %reshape.784), calls=%async_computation.1 | async-start | bytes 393216 | tf_op jit(solution)/shard_map/all_to_all | solution.py:131
  98.6 8.8 %collective-permute-start.2 = (bf16[1,3,128]{2,1,0:T(4,128)(2,1)}, bf16[1,3,128]{2,1,0:T(4,128)(2,1)}, u32[]{:S(2)}, u32[]{:S(2)}) collective-permute-start(bf16[1,3,128]{2,1,0:T(4,128)(2,1)} %slice.318), channel_id=1, source_target_pairs={{0,1},{1,2},{2,3},{3,4},{4,5},{5,6},{6,7},{7,8},{8,9},{9,10},{10,1... | collective-permute-start | bytes 2312 | tf_op jit(solution)/shard_map/ppermute | solution.py:26
  104.8 5.7 %copy-start.12 = (f32[8,8]{0,1:T(8,128)S(1)}, f32[8,8]{0,1:T(8,128)}, u32[]{:S(2)}) copy-start(f32[8,8]{0,1:T(8,128)} %convolution_bitcast_fusion) | copy-start | bytes 772
  104.8 48.8 %copy-start.7 = (f32[8,32,3,128]{3,1,2,0:T(8,128)S(1)}, f32[8,32,3,128]{3,1,2,0:T(8,128)}, u32[]{:S(2)}) copy-start(f32[8,32,3,128]{3,1,2,0:T(8,128)} %param.28) | copy-start | bytes 1179652
  106.0 48.2 %copy-start.8 = (f32[32,3,128]{2,0,1:T(8,128)S(1)}, f32[32,3,128]{2,0,1:T(8,128)}, u32[]{:S(2)}) copy-start(f32[32,3,128]{2,0,1:T(8,128)} %param.26) | copy-start | bytes 147460
  107.2 53.3 %copy-start.15 = (s32[64]{0:T(128)S(1)}, s32[64]{0:T(128)}, u32[]{:S(2)}) copy-start(s32[64]{0:T(128)} %copy-done.14) | copy-start | bytes 772
  155.2 13.0 %all-to-all-start.2 = ((bf16[32,4,384]{2,1,0:T(4,128)(2,1)}), bf16[32,4,384]{2,1,0:T(4,128)(2,1)S(1)}, u32[]{:S(2)}, u32[]{:S(2)}) async-start(bf16[32,4,384]{2,1,0:T(4,128)(2,1)} %reshape.787), calls=%async_computation.2 | async-start | bytes 196608 | tf_op jit(solution)/shard_map/all_to_all | solution.py:180
where the time goes:
time: 172 us; the launch traced here: 171 us
  local copies, waits for them, and re-layouts  66.3 us (39%)
  blocking collectives  40 us (23%)
  starting transfers between devices  23.6 us (14%)
  other arithmetic  20.4 us (12%)
  matrix products  9.77 us (6%)
  waiting for transfers between devices  9.52 us (6%)
    gather x1, local copies, waits for them, and re-layouts, on_device(): wall_row[correlation][:, None, :] * normals  51.2 us
    psum x1, blocking collectives, on_device(): lax.psum((gram_local, projected_local), ('group', 'dev'))  40 us
    all_to_all x1, waiting for transfers between devices, on_device(): lax.all_to_all(replies.reshape(peer_count, capacity, width_row), ('group'...  7.1 us
    ppermute x1, starting transfers between devices, extended(): after = lax.ppermute(leading, axis, down)  6.4 us
    all_to_all x1, starting transfers between devices, on_device(): lax.all_to_all(send_tag.reshape(peer_count, capacity), ('group', 'dev'),...  5.7 us
    all_to_all x1, starting transfers between devices, on_device(): lax.all_to_all(replies.reshape(peer_count, capacity, width_row), ('group'...  5.25 us
    sub x3, other arithmetic, rusanov(): 0.5 * (flux_left + flux_right)  3.7 us
    all_to_all x1, starting transfers between devices, on_device(): lax.all_to_all(send_loads.reshape(peer_count, capacity, width_row), ('gro...  3.57 us
  transfers between devices with their start and end apart: 6, of which 2 were waited for; matrix products, arithmetic and copies ran while one was open for 47% of the time, Pallas kernels for 0%

commit v1 on v0

--- a/solution.py
+++ b/solution.py
@@ -166,7 +166,9 @@
         "mbcj,bcj->m", diff_res, coupling_res, precision=lax.Precision.HIGHEST
     )
     gram_local = jnp.einsum("mbcj,nbcj->mn", diff_res, diff_res, precision=lax.Precision.HIGHEST)
-    gram_matrix, projected = lax.psum((gram_local, projected_local), ("group", "dev"))
+    gram_matrix, projected = lax.psum(
+        lax.psum((gram_local, projected_local), "dev"), axis_name="group"
+    )
     mixing = -cho_apply(gram_matrix, projected)
     disp_next = (
         displacement

time: 172 us -> 156 us (0.907)
  blocking collectives: 40 us -> 26.8 us
  starting transfers between devices: 23.6 us -> 20.9 us
    psum x1 -> x2, blocking collectives: 40 us -> 26.8 us  [the longest x1 17.7 us: on_device(): lax.psum((gram_local, projected_local), 'dev')]
    all_to_all x1, starting transfers between devices: 5.25 us -> 2.57 us  [on_device(): lax.all_to_all(replies.reshape(peer_count, capacity, width_row), ('group'...]
  transfers between devices with their start and end apart: 6 -> 6, of which waited for: 2 -> 2; matrix products, arithmetic and copies ran while one was open for 47% -> 51% of each run, Pallas kernels for 0% -> 0%
where the time goes in v1:
time: 156 us; the launch traced here: 155 us
  local copies, waits for them, and re-layouts  66.3 us (42%)
  blocking collectives  26.8 us (17%)
  starting transfers between devices  20.9 us (13%)
  other arithmetic  20.4 us (13%)
  matrix products  9.77 us (6%)
  waiting for transfers between devices  9.52 us (6%)
    gather x1, local copies, waits for them, and re-layouts, on_device(): wall_row[correlation][:, None, :] * normals  51.2 us
    psum x1, blocking collectives, on_device(): lax.psum((gram_local, projected_local), 'dev')  17.7 us
    psum x1, blocking collectives, on_device(): lax.psum(lax.psum((gram_local, projected_local), 'dev'), axis_name='group')  9.07 us
    all_to_all x1, waiting for transfers between devices, on_device(): lax.all_to_all(replies.reshape(peer_count, capacity, width_row), ('group'...  7.1 us
    ppermute x1, starting transfers between devices, extended(): after = lax.ppermute(leading, axis, down)  6.4 us
    all_to_all x1, starting transfers between devices, on_device(): lax.all_to_all(send_tag.reshape(peer_count, capacity), ('group', 'dev'),...  5.7 us
    sub x3, other arithmetic, rusanov(): 0.5 * (flux_left + flux_right)  3.7 us
    all_to_all x1, starting transfers between devices, on_device(): lax.all_to_all(send_loads.reshape(peer_count, capacity, width_row), ('gro...  3.57 us
  transfers between devices with their start and end apart: 6, of which 2 were waited for; matrix products, arithmetic and copies ran while one was open for 51% of the time, Pallas kernels for 0%

profile of v1, /device:TPU:0, one launch (start us, length us, event | category | flops | bytes accessed | tf_op | source)
XLA Modules:
  0.0 154.9 jit_solution(5394172058144224771)
XLA Ops:
  0.7 1.4 multiply_reduce_fusion.5
  2.0 0.7 bitcast_dynamic-update-slice_fusion.1
  2.8 0.7 fusion.55
  3.4 0.7 fusion.54
  4.2 0.9 pad_maximum_fusion.3
  5.1 6.4 %collective-permute-start.1 = (f32[5,1,320,128]{3,2,1,0:T(8,128)}, f32[5,1,320,128]{3,2,1,0:T(8,128)}, u32[]{:S(2)}, u32[]{:S(2)}) collective-permute-start(f32[5,1,320,128]{3,2,1,0:T(8,128)} %pad_maximum_fusion.3), channel_id=1, source_target_pairs={{1,0},{2,1},{3,2},{4,3},{5,4},{6,5},{7,6},{8,7},{9,8},{10,9},{11,1... | collective-permute-start | bytes 2457608 | tf_op jit(solution)/shard_map/ppermute | solution.py:18
  11.9 0.8 scatter_custom_fusion
  12.7 0.7 all_to_all.12
  13.4 5.7 %all-to-all-start = ((f32[32,1,4]{2,1,0:T(1,128)}), f32[32,1,4]{2,1,0:T(1,128)S(1)}, u32[]{:S(2)}, u32[]{:S(2)}) async-start(f32[32,1,4]{2,1,0:T(1,128)} %bitcast.30), calls=%async_computation | async-start | bytes 32768 | tf_op jit(solution)/shard_map/all_to_all | solution.py:138
  19.1 0.7 slice.284
  19.8 1.2 slice.283
  21.1 1.7 %fusion.107 = (f32[5,1,320,1]{3,2,1,0:T(8,128)S(1)}, f32[5,1,320,1]{3,2,1,0:T(8,128)S(1)}) fusion(f32[5,1,320,128]{3,2,1,0:T(8,128)} %pad_maximum_fusion.3, f32[5]{0:T(128)S(1)} %copy-done.16), kind=kLoop, calls=%fused_computation.214 | loop fusion | flops 1600 | bytes 25620 | tf_op jit(solution)/shard_map/slice | solution.py:65
  24.4 0.7 fusion.50
  25.2 0.8 copy-done.4
  26.3 0.8 bitcast_dynamic-update-slice_fusion
  27.1 1.4 fusion.6
  28.6 0.6 multiply_subtract_fusion
  29.2 2.4 %collective-permute-done = f32[5,1,320,128]{3,2,1,0:T(8,128)} collective-permute-done((f32[5,1,320,128]{3,2,1,0:T(8,128)}, f32[5,1,320,128]{3,2,1,0:T(8,128)}, u32[]{:S(2)}, u32[]{:S(2)}) %collective-permute-start) | collective-permute-done | bytes 819232 | tf_op jit(solution)/shard_map/ppermute | solution.py:17
  31.6 1.7 %pad_maximum_fusion.1 = (f32[5,2,320,128]{3,2,1,0:T(8,128)S(1)}, f32[5,2,320,128]{3,2,1,0:T(8,128)S(1)}) fusion(f32[5,1,320,128]{3,2,1,0:T(8,128)} %collective-permute-done.1, f32[1,1,320,128]{3,2,1,0:T(8,128)S(1)} %bitcast.216, f32[3,1,320,128]{3,2,1,0:T(8,128)S(1)} %get-tuple-element.50, f32[1,1,320,128]{3,2,1,0:T(8,128)S(1)} %bitcast.209, ...), kind=kLoop, calls=%fused_computation.12 | loop fusion | flops 2457600 | bytes 5734400 | tf_op jit(solution)/shard_map/concatenate | solution.py:19
  34.6 1.7 %multiply_subtract_fusion.1 = f32[5,2,320,128]{3,2,1,0:T(8,128)S(1)} fusion(f32[5,2,320,128]{3,2,1,0:T(8,128)S(1)} %multiply_dynamic-update-slice_fusion.6, f32[5,2,320,128]{3,2,1,0:T(8,128)S(1)} %multiply_dynamic-update-slice_fusion.4, f32[2,320,128]{2,1,0:T(8,128)S(1)} %get-tuple-element.20, f32[5,1,320,128]{3,2,1,0:T(8,128)} %collective-permute-done.1, ...), kind=kLoop, calls=%fused_computation.16 | loop fusion | flops 4505600 | bytes 7700480 | tf_op jit(solution)/shard_map/sub | solution.py:48
  37.6 51.2 %gather_fusion = f32[8192]{0:T(1024)S(1)} fusion(f32[320]{0:T(512)S(1)} %subtract_multiply_fusion, s32[8192]{0:T(1024)S(1)} %fusion.78), kind=kCustom, calls=%fused_computation | custom fusion | bytes 98304 | tf_op jit(solution)/shard_map/gather | solution.py:107
  88.9 1.3 fusion.74
  90.2 1.8 %scatter_custom_fusion.1 = f32[128,384]{1,0:T(8,128)} fusion(s32[64]{0:T(128)} %copy-done.14, f32[8,8,3,128]{3,2,1,0:T(4,128)} %bitcast.223, f32[]{:T(128)} %constant.80.clone.1), kind=kCustom, calls=%fused_computation.164 | custom fusion | bytes 328192 | tf_op jit(solution)/shard_map/scatter | solution.py:125
  92.0 1.7 %reshape.784 = f32[32,4,384]{2,1,0:T(4,128)} reshape(f32[128,384]{1,0:T(8,128)} %scatter_custom_fusion.1) | data formatting | bytes 393216 | tf_op jit(solution)/shard_map/reshape | solution.py:132
  93.7 3.6 %all-to-all-start.1 = ((f32[32,4,384]{2,1,0:T(4,128)}), f32[32,4,384]{2,1,0:T(4,128)}, u32[]{:S(2)}, u32[]{:S(2)}) async-start(f32[32,4,384]{2,1,0:T(4,128)} %reshape.784), calls=%async_computation.1 | async-start | bytes 393216 | tf_op jit(solution)/shard_map/all_to_all | solution.py:131
  97.2 0.8 copy.93
  98.6 2.7 %collective-permute-start.2 = (bf16[1,3,128]{2,1,0:T(4,128)(2,1)}, bf16[1,3,128]{2,1,0:T(4,128)(2,1)}, u32[]{:S(2)}, u32[]{:S(2)}) collective-permute-start(bf16[1,3,128]{2,1,0:T(4,128)(2,1)} %slice.318), channel_id=1, source_target_pairs={{0,1},{1,2},{2,3},{3,4},{4,5},{5,6},{6,7},{7,8},{8,9},{9,10},{10,1... | collective-permute-start | bytes 2312 | tf_op jit(solution)/shard_map/ppermute | solution.py:26
  101.3 0.6 slice.319
  101.9 1.6 %convolution_bitcast_fusion = f32[8,8]{0,1:T(8,128)} fusion(f32[8,32,3,128]{3,1,2,0:T(8,128)S(1)} %copy-done.5), kind=kOutput, calls=%fused_computation.21 | convolution fusion | flops 9437184 | bytes 393472 | tf_op jit(solution)/shard_map/mbcj,nbcj->mn/dot_general | solution.py:168
  103.5 1.3 fusion.108
  105.3 0.6 reduce.20
  106.1 1.0 reshape.785
  107.4 1.9 %fusion.1 = f32[32,3,128]{2,1,0:T(4,128)S(1)} fusion(f32[32,3,128]{2,1,0:T(4,128)} %fusion.108, bf16[32,128,128]{2,1,0:T(8,128)(2,1)} %param.24, f32[32,3,128]{2,0,1:T(8,128)S(1)} %fusion.87, f32[32,3,128]{2,0,1:T(8,128)} %param.25, bf16[31,3,128]{2,1,0:T(4,128)(2,1)} %slice.319, bf16[1,3,128]{2,1,0:T(4,128)(2,1)} %collective-permute-done.2), kind=kOutput, calls=%fused_computation.20 | convolution fusion | flops 3244032 | bytes 1269760 | tf_op jit(solution)/shard_map/bcj,bij->bci/dot_general | solution.py:161
  109.4 1.1 convolution_bitcast_fusion.3
  110.5 17.7 %all-reduce = (f32[8,8]{0,1:T(8,128)S(1)}, f32[8]{0:T(128)S(1)}) all-reduce(f32[8,8]{0,1:T(8,128)S(1)} %copy-done.12, f32[8]{0:T(128)S(1)} %convolution_bitcast_fusion.3), channel_id=1, replica_groups=mesh['group'=4,'dev'=8] {'dev'}, use_global_device_ids=true, to_apply=%region_12.13 | all-reduce | flops 72 | bytes 576 | tf_op jit(solution)/shard_map/psum | solution.py:170
  128.3 9.1 %all-reduce.1 = (f32[8,8]{0,1:T(8,128)S(1)}, f32[8]{0:T(128)S(1)}) all-reduce(f32[8,8]{0,1:T(8,128)S(1)} %get-tuple-element.14, f32[8]{0:T(128)S(1)} %get-tuple-element.15), channel_id=1, replica_groups=mesh['group'=4,'dev'=8] {'group'}, use_global_device_ids=true, to_apply=%region_13.14 | all-reduce | flops 72 | bytes 576 | tf_op jit(solution)/shard_map/psum | solution.py:169
  137.4 0.7 cholesky.16
  138.2 0.6 compare_reduce_fusion
  138.8 0.6 fusion.90
  139.5 0.6 custom-call.8
  140.4 0.7 fusion.14
  141.3 0.7 reshape.787
  142.0 2.6 %all-to-all-start.2 = ((bf16[32,4,384]{2,1,0:T(4,128)(2,1)}), bf16[32,4,384]{2,1,0:T(4,128)(2,1)S(1)}, u32[]{:S(2)}, u32[]{:S(2)}) async-start(bf16[32,4,384]{2,1,0:T(4,128)(2,1)} %reshape.787), calls=%async_computation.2 | async-start | bytes 196608 | tf_op jit(solution)/shard_map/all_to_all | solution.py:182
  144.6 0.6 copy.55
  145.2 7.1 %all-to-all-done.2 = bf16[32,4,384]{2,1,0:T(4,128)(2,1)S(1)} async-done(((bf16[32,4,384]{2,1,0:T(4,128)(2,1)}), bf16[32,4,384]{2,1,0:T(4,128)(2,1)S(1)}, u32[]{:S(2)}, u32[]{:S(2)}) %all-to-all-start.2) | async-done | bytes 98336 | tf_op jit(solution)/shard_map/all_to_all | solution.py:182
  152.4 0.7 gather_fusion.1
  153.1 1.2 fusion.109
  154.3 0.7 copy.56
  (99 shorter events, 7.2 us)
Async XLA Ops:
  0.6 88.2 %copy-start = (bf16[64,128,128]{2,1,0:T(8,128)(2,1)S(1)}, bf16[64,128,128]{2,1,0:T(8,128)(2,1)}, u32[]{:S(2)}) copy-start(bf16[64,128,128]{2,1,0:T(8,128)(2,1)} %param.18) | copy-start | bytes 6291460
  0.6 1.4 copy-start.1
  0.7 2.8 %copy-start.9 = (f32[1,320,128]{2,1,0:T(8,128)S(1)}, f32[1,320,128]{2,1,0:T(8,128)}, u32[]{:S(2)}) copy-start(f32[1,320,128]{2,1,0:T(8,128)} %param.17) | copy-start | bytes 491524
  2.0 3.1 %copy-start.3 = (f32[320,128]{1,0:T(8,128)}, f32[320,128]{1,0:T(8,128)S(1)}, u32[]{:S(2)}) copy-start(f32[320,128]{1,0:T(8,128)S(1)} %get-tuple-element.31) | copy-start | bytes 491524
  2.7 8.8 %copy-start.13 = (s32[64,1]{0,1:T(1,128)S(1)}, s32[64,1]{0,1:T(1,128)}, u32[]{:S(2)}) copy-start(s32[64,1]{0,1:T(1,128)} %param.21) | copy-start | bytes 772
  3.4 8.4 %copy-start.17 = (s32[64]{0:T(128)S(1)}, s32[64]{0:T(128)}, u32[]{:S(2)}) copy-start(s32[64]{0:T(128)} %param.22) | copy-start | bytes 772
  4.2 16.9 %copy-start.16 = (f32[5]{0:T(128)S(1)}, f32[5]{0:T(128)}, u32[]{:S(2)}) copy-start(f32[5]{0:T(128)} %constant.91.clone) | copy-start | bytes 64
  5.1 24.1 %collective-permute-start.1 = (f32[5,1,320,128]{3,2,1,0:T(8,128)}, f32[5,1,320,128]{3,2,1,0:T(8,128)}, u32[]{:S(2)}, u32[]{:S(2)}) collective-permute-start(f32[5,1,320,128]{3,2,1,0:T(8,128)} %pad_maximum_fusion.3), channel_id=1, source_target_pairs={{1,0},{2,1},{3,2},{4,3},{5,4},{6,5},{7,6},{8,7},{9,8},{10,9},{11,1... | collective-permute-start | bytes 2457608 | tf_op jit(solution)/shard_map/ppermute | solution.py:18
  11.5 20.1 %collective-permute-start = (f32[5,1,320,128]{3,2,1,0:T(8,128)}, f32[5,1,320,128]{3,2,1,0:T(8,128)}, u32[]{:S(2)}, u32[]{:S(2)}) collective-permute-start(f32[5,1,320,128]{3,2,1,0:T(8,128)} %pad_maximum_fusion.3), channel_id=1, source_target_pairs={{0,1},{1,2},{2,3},{3,4},{4,5},{5,6},{6,7},{7,8},{8,9},{9,10},{10,1... | collective-permute-start | bytes 2457608 | tf_op jit(solution)/shard_map/ppermute | solution.py:17
  11.9 10.9 %copy-start.14 = (s32[64]{0:T(128)}, s32[64]{0:T(128)S(1)}, u32[]{:S(2)}) copy-start(s32[64]{0:T(128)S(1)} %fusion.94) | copy-start | bytes 772
  13.4 80.2 %all-to-all-start = ((f32[32,1,4]{2,1,0:T(1,128)}), f32[32,1,4]{2,1,0:T(1,128)S(1)}, u32[]{:S(2)}, u32[]{:S(2)}) async-start(f32[32,1,4]{2,1,0:T(1,128)} %bitcast.30), calls=%async_computation | async-start | bytes 32768 | tf_op jit(solution)/shard_map/all_to_all | solution.py:138
  25.1 0.9 copy-start.4
  27.1 1.5 copy-start.11
  36.7 0.9 copy-start.2
  37.6 51.2 %copy-start.10 = (f32[64,3,128]{2,0,1:T(8,128)S(1)}, f32[64,3,128]{2,0,1:T(8,128)}, u32[]{:S(2)}) copy-start(f32[64,3,128]{2,0,1:T(8,128)} %param.20) | copy-start | bytes 294916
  88.9 13.1 %copy-start.5 = (f32[8,32,3,128]{3,1,2,0:T(8,128)S(1)}, f32[8,32,3,128]{3,1,2,0:T(8,128)}, u32[]{:S(2)}) copy-start(f32[8,32,3,128]{3,1,2,0:T(8,128)} %param.27) | copy-start | bytes 1179652
  88.9 14.6 %copy-start.6 = (bf16[32,128,128]{2,1,0:T(8,128)(2,1)S(1)}, bf16[32,128,128]{2,1,0:T(8,128)(2,1)}, u32[]{:S(2)}) copy-start(bf16[32,128,128]{2,1,0:T(8,128)(2,1)} %param.23) | copy-start | bytes 3145732
  93.7 12.4 %all-to-all-start.1 = ((f32[32,4,384]{2,1,0:T(4,128)}), f32[32,4,384]{2,1,0:T(4,128)}, u32[]{:S(2)}, u32[]{:S(2)}) async-start(f32[32,4,384]{2,1,0:T(4,128)} %reshape.784), calls=%async_computation.1 | async-start | bytes 393216 | tf_op jit(solution)/shard_map/all_to_all | solution.py:131
  98.6 8.8 %collective-permute-start.2 = (bf16[1,3,128]{2,1,0:T(4,128)(2,1)}, bf16[1,3,128]{2,1,0:T(4,128)(2,1)}, u32[]{:S(2)}, u32[]{:S(2)}) collective-permute-start(bf16[1,3,128]{2,1,0:T(4,128)(2,1)} %slice.318), channel_id=1, source_target_pairs={{0,1},{1,2},{2,3},{3,4},{4,5},{5,6},{6,7},{7,8},{8,9},{9,10},{10,1... | collective-permute-start | bytes 2312 | tf_op jit(solution)/shard_map/ppermute | solution.py:26
  104.8 5.7 %copy-start.12 = (f32[8,8]{0,1:T(8,128)S(1)}, f32[8,8]{0,1:T(8,128)}, u32[]{:S(2)}) copy-start(f32[8,8]{0,1:T(8,128)} %convolution_bitcast_fusion) | copy-start | bytes 772
  104.8 35.6 %copy-start.7 = (f32[8,32,3,128]{3,1,2,0:T(8,128)S(1)}, f32[8,32,3,128]{3,1,2,0:T(8,128)}, u32[]{:S(2)}) copy-start(f32[8,32,3,128]{3,1,2,0:T(8,128)} %param.28) | copy-start | bytes 1179652
  106.0 35.0 %copy-start.8 = (f32[32,3,128]{2,0,1:T(8,128)S(1)}, f32[32,3,128]{2,0,1:T(8,128)}, u32[]{:S(2)}) copy-start(f32[32,3,128]{2,0,1:T(8,128)} %param.26) | copy-start | bytes 147460
  107.2 37.4 %copy-start.15 = (s32[64]{0:T(128)S(1)}, s32[64]{0:T(128)}, u32[]{:S(2)}) copy-start(s32[64]{0:T(128)} %copy-done.14) | copy-start | bytes 772
  142.0 10.3 %all-to-all-start.2 = ((bf16[32,4,384]{2,1,0:T(4,128)(2,1)}), bf16[32,4,384]{2,1,0:T(4,128)(2,1)S(1)}, u32[]{:S(2)}, u32[]{:S(2)}) async-start(bf16[32,4,384]{2,1,0:T(4,128)(2,1)} %reshape.787), calls=%async_computation.2 | async-start | bytes 196608 | tf_op jit(solution)/shard_map/all_to_all | solution.py:182
